TPU v7x, 128 devices: a whole 4x4x4 slice. The times are simulated.
128 devices in a mesh: seq: 16 (over y, z_hi, core), head: 8 (over z_lo, x).
Axes of the slice: x: 4, y: 4, z: 4 (z_hi: 2, z_lo: 2; z = z_hi * 2 + z_lo), core: 2. Of those that a mesh axis runs over, the one named last changes fastest.
Arguments:
- enc_in: bfloat16 [8192, 4, 768], P(('seq', 'head')), may hold values from -6 to 6
- conv_weight: bfloat16 [5, 768, 1536], replicated, may hold values from -0.09375 to 0.09375
- norm_gain: float32 [1536], replicated, may hold values from 0.25 to 1.75
- w_qkv: bfloat16 [3, 1536, 1536], P(None, None, 'head'), may hold values from -0.63788795 to 0.63788795
- w_out: bfloat16 [1536, 1536], P('head'), may hold values from -0.15625 to 0.15625
- grad_out: bfloat16 [4096, 4, 1536], P(('seq', 'head')), may hold values from -6 to 6
Outputs:
- mixed: bfloat16 [4096, 4, 1536], P(('seq', 'head'))
- grad_input: bfloat16 [8192, 4, 768], P(('seq', 'head'))
- grad_w_qkv: float32 [3, 1536, 1536], P(None, None, 'head')
- grad_w_out: float32 [1536, 1536], P('head')
All inputs are finite; a program needn't handle non-finite values.
Results may differ from a plain program's by a relative error of at most 0.024.
Values may be sent and summed in bfloat16 or wider, within the bound.
A program may use at most 256 MiB of HBM per device.

v0:
```python
import jax
import jax.numpy as jnp
from jax import lax
from jax.sharding import PartitionSpec as P

DH = 192
KW = 5


def padded_2(block, sides, width):
    for axis, dim in sides:
        count = lax.axis_size(axis)
        forward = [(i, i + 1) for i in range(count - 1)]
        backward = [(target, source) for source, target in forward]
        low = lax.ppermute(
            lax.slice_in_dim(block, block.shape[dim] - width, None, axis=dim), axis, forward
        )
        high = lax.ppermute(lax.slice_in_dim(block, 0, width, axis=dim), axis, backward)
        block = jnp.concatenate([low, block, high], axis=dim)
    return block


def body(enc_in, conv_weight, norm_gain, w_qkv, w_out, grad_out):
    fine_rows = enc_in.shape[0]
    slab_rows = fine_rows // 2
    seq_count = enc_in.shape[1]
    out_width = conv_weight.shape[2]
    local_width = w_qkv.shape[2]
    local_heads = local_width // DH
    logit_scale = DH ** (-0.5)
    padded = padded_2(enc_in, ((("seq", "head"), 0),), 2)
    convolved = jnp.zeros((fine_rows, seq_count, out_width), jnp.float32)
    for offset in range(KW):
        convolved = convolved + jnp.einsum(
            "tbi,io->tbo",
            padded[offset : offset + fine_rows],
            conv_weight[offset],
            preferred_element_type=jnp.float32,
        )
    activated, gelu_pull = jax.vjp(jax.nn.gelu, convolved)
    skip = jnp.mean(activated.reshape(slab_rows, 2, seq_count, out_width), axis=1).astype(
        jnp.bfloat16
    )
    skip_wide = skip.astype(jnp.float32)
    inv_rms = lax.rsqrt(jnp.mean(skip_wide * skip_wide, axis=-1, keepdims=True) + 1e-06)
    normed = (skip_wide * inv_rms * norm_gain).astype(jnp.bfloat16)
    normed_rows = lax.all_gather(normed, "head", axis=0, tiled=True)
    grad_rows = lax.all_gather(grad_out, "head", axis=0, tiled=True)
    tower_rows = normed_rows.shape[0]
    qkv = jnp.einsum(
        "tbc,ice->itbe", normed_rows, w_qkv, preferred_element_type=jnp.float32
    ).astype(jnp.bfloat16)
    qkv = qkv.reshape(3, tower_rows, seq_count, local_heads, DH)
    query_matrix, key_matrix, value_matrix = (qkv[0], qkv[1], qkv[2])
    key_all, value_all = (
        lax.all_gather(key_matrix, "seq", axis=0, tiled=True),
        lax.all_gather(value_matrix, "seq", axis=0, tiled=True),
    )
    attention_logits = (
        jnp.einsum("qbhd,kbhd->bhqk", query_matrix, key_all, preferred_element_type=jnp.float32)
        * logit_scale
    )
    row_peak = jnp.max(attention_logits, axis=-1, keepdims=True)
    exponent = jnp.exp(attention_logits - row_peak)
    row_total = jnp.sum(exponent, axis=-1, keepdims=True)
    soft_weights = exponent / row_total
    narrow_probabilities = soft_weights.astype(jnp.bfloat16)
    attention_output = jnp.einsum(
        "bhqk,kbhd->qbhd", narrow_probabilities, value_all, preferred_element_type=jnp.float32
    )
    o_narrow = attention_output.reshape(tower_rows, seq_count, local_width).astype(jnp.bfloat16)
    piece = o_narrow
    head_sum = lax.psum_scatter(
        jnp.einsum("tbe,ec->tbc", piece, w_out, preferred_element_type=jnp.float32).astype(
            jnp.bfloat16
        ),
        "head",
        scatter_dimension=0,
        tiled=True,
    ).astype(jnp.float32)
    mixed = (skip_wide + head_sum).astype(jnp.bfloat16)
    part_w_out = jnp.einsum("tbe,tbc->ec", o_narrow, grad_rows, preferred_element_type=jnp.float32)
    d_out = jnp.einsum("tbc,ec->tbe", grad_rows, w_out, preferred_element_type=jnp.float32).astype(
        jnp.bfloat16
    )
    d_out = d_out.reshape(tower_rows, seq_count, local_heads, DH)
    delta = jnp.sum(d_out.astype(jnp.float32) * attention_output, axis=-1)
    probability_gradient = jnp.einsum(
        "qbhd,kbhd->bhqk", d_out, value_all, preferred_element_type=jnp.float32
    )
    d_scores = soft_weights * (probability_gradient - jnp.transpose(delta, (1, 2, 0))[..., None])
    narrow_gradient = d_scores.astype(jnp.bfloat16)
    query_gradient = logit_scale * jnp.einsum(
        "bhqk,kbhd->qbhd", narrow_gradient, key_all, preferred_element_type=jnp.float32
    )
    key_terms = logit_scale * jnp.einsum(
        "bhqk,qbhd->kbhd", narrow_gradient, query_matrix, preferred_element_type=jnp.float32
    )
    value_terms = jnp.einsum(
        "bhqk,qbhd->kbhd", narrow_probabilities, d_out, preferred_element_type=jnp.float32
    )
    d_keys, d_values = (
        lax.psum_scatter(
            key_terms.astype(jnp.bfloat16), "seq", scatter_dimension=0, tiled=True
        ).astype(jnp.float32),
        lax.psum_scatter(
            value_terms.astype(jnp.bfloat16), "seq", scatter_dimension=0, tiled=True
        ).astype(jnp.float32),
    )
    dqkv = (
        jnp.stack([query_gradient, d_keys, d_values])
        .reshape(3, tower_rows, seq_count, local_width)
        .astype(jnp.bfloat16)
    )
    part_w_qkv = jnp.einsum("tbc,itbe->ice", normed_rows, dqkv, preferred_element_type=jnp.float32)
    piece = dqkv
    d_normed = lax.psum_scatter(
        jnp.einsum("itbe,ice->tbc", piece, w_qkv, preferred_element_type=jnp.float32).astype(
            jnp.bfloat16
        ),
        "head",
        scatter_dimension=0,
        tiled=True,
    ).astype(jnp.float32)
    unit_rows = skip_wide * inv_rms
    scaled = d_normed * norm_gain
    d_skip = grad_out.astype(jnp.float32) + inv_rms * (
        scaled - unit_rows * jnp.mean(scaled * unit_rows, axis=-1, keepdims=True)
    )
    d_act = jnp.repeat(d_skip, 2, axis=0) * 0.5
    d_conv = gelu_pull(d_act)[0].astype(jnp.bfloat16)
    d_pad = padded_2(d_conv, ((("seq", "head"), 0),), 2)
    grad_input = jnp.zeros((fine_rows, seq_count, enc_in.shape[2]), jnp.float32)
    for offset in range(KW):
        grad_input = grad_input + jnp.einsum(
            "tbo,io->tbi",
            d_pad[4 - offset : 4 - offset + fine_rows],
            conv_weight[offset],
            preferred_element_type=jnp.float32,
        )
    grad_w_qkv, grad_w_out = (
        lax.psum(part_w_qkv.astype(jnp.bfloat16), "seq").astype(jnp.float32),
        lax.psum(part_w_out.astype(jnp.bfloat16), "seq").astype(jnp.float32),
    )
    return (mixed, grad_input.astype(jnp.bfloat16), grad_w_qkv, grad_w_out)


def solution(mesh):
    return jax.shard_map(
        body,
        mesh=mesh,
        in_specs=(
            P(("seq", "head"), None, None),
            P(),
            P(),
            P(None, None, "head"),
            P("head", None),
            P(("seq", "head"), None, None),
        ),
        out_specs=(
            P(("seq", "head"), None, None),
            P(("seq", "head"), None, None),
            P(None, None, "head"),
            P("head", None),
        ),
        check_vma=False,
    )
```

profile of v0, /device:TPU:16, one launch (start us, length us, event | category | flops | bytes accessed | tf_op | source)
XLA Modules:
  0.0 745.7 jit_solution(13010598031011791318)
XLA Ops:
  8.4 7.5 %collective-permute-start.1 = (bf16[2,4,768]{2,0,1:T(2,128)(2,1)S(1)}, bf16[2,4,768]{2,0,1:T(2,128)(2,1)S(1)}, u32[]{:S(2)}, u32[]{:S(2)}) collective-permute-start(bf16[2,4,768]{2,0,1:T(2,128)(2,1)S(1)} %get-tuple-element.19), channel_id=1, source_target_pairs={{1,0},{2,1},{3,2},{4,3},{5,4},{6,5},{7,6},{8,7},{9,8},{10,9},{11,1... | collective-permute-start | bytes 36872 | tf_op jit(solution)/shard_map/ppermute | solution.py:18
  17.8 2.6 fusion.33
  30.1 4.4 multiply_multiply_fusion.2
  36.7 2.9 reduce_sum.47
  42.9 43.0 %all-gather.7.cloned.1.call-done = bf16[256,4,1536]{2,0,1:T(8,128)(2,1)} async-done(((bf16[32,4,1536]{2,0,1:T(8,128)(2,1)}), bf16[256,4,1536]{2,0,1:T(8,128)(2,1)}) %all-gather.7.cloned.1.call-update) | async-done | bytes 3145744 | tf_op jit(solution)/shard_map/all_gather | solution.py:47
  85.9 3.9 fusion.66
  91.6 40.5 %all-gather.9.cloned.1.call-done = bf16[256,4,1536]{2,0,1:T(8,128)(2,1)} async-done(((bf16[32,4,1536]{2,0,1:T(8,128)(2,1)}), bf16[256,4,1536]{2,0,1:T(8,128)(2,1)}) %all-gather.9.cloned.1.call-update) | async-done | bytes 3145744 | tf_op jit(solution)/shard_map/all_gather | solution.py:48
  132.0 3.9 convolution_convert_fusion.2
  135.9 66.5 %all-gather.13.cloned.1.call-done = bf16[1,4096,4,192]{1,3,0,2:T(8,128)(2,1)} async-done(((bf16[1,256,4,192]{1,3,0,2:T(8,128)(2,1)}), bf16[1,4096,4,192]{1,3,0,2:T(8,128)(2,1)}) %all-gather.13.cloned.1.call-update) | async-done | bytes 6291472 | tf_op jit(solution)/shard_map/all_gather | solution.py:56
  202.4 10.9 %fusion.8 = f32[4,256,4096]{2,1,0:T(8,128)} fusion(bf16[1,4096,4,192]{1,3,0,2:T(8,128)(2,1)} %all-gather.13.cloned.1.call-done, bf16[3,256,4,192]{1,3,0,2:T(8,128)(2,1)S(1)} %fusion.66), kind=kOutput, calls=%fused_computation.13 | convolution fusion | flops 1610612736 | bytes 23461888 | tf_op jit(solution)/shard_map/qbhd,kbhd->bhqk/dot_general | solution.py:60
  213.3 18.3 %fusion.141 = (f32[4,256]{1,0:T(4,128)S(1)}, f32[4,256,4096]{2,1,0:T(8,128)}) fusion(f32[4,256,4096]{2,1,0:T(8,128)} %fusion.8), kind=kOutput, calls=%fused_computation.145 | output fusion | flops 16781312 | bytes 33558528 | tf_op jit(solution)/shard_map/sub | solution.py:64
  231.6 6.9 fusion.5
  238.6 3.2 copy-done.1
  241.8 4.5 fusion.13
  246.6 26.5 %all-gather.11.cloned.1.call-done = bf16[1,4096,4,192]{1,3,0,2:T(8,128)(2,1)} async-done(((bf16[1,256,4,192]{1,3,0,2:T(8,128)(2,1)}), bf16[1,4096,4,192]{1,3,0,2:T(8,128)(2,1)}) %all-gather.11.cloned.1.call-update) | async-done | bytes 6291472 | tf_op jit(solution)/shard_map/all_gather | solution.py:57
  273.1 8.9 %fusion.115 = (f32[256,4]{0,1:T(4,128)S(1)}, bf16[256,4,1,192]{0,3,1,2:T(8,128)(2,1)}) fusion(bf16[256,4,192]{0,2,1:T(8,128)(2,1)} %convolution_convert_fusion.2, bf16[4,256,4096]{2,1,0:T(8,128)(2,1)} %copy-done.1, bf16[1,4096,4,192]{1,3,0,2:T(8,128)(2,1)} %all-gather.11.cloned.1.call-done), kind=kOutput, calls=%fused_computation.110 | convolution fusion | flops 1611398144 | bytes 15470592 | tf_op jit(solution)/shard_map/bhqk,kbhd->qbhd/dot_general | solution.py:68
  282.0 10.3 %multiply_convert_fusion = bf16[4,256,4096]{2,1,0:T(8,128)(2,1)S(1)} fusion(bf16[256,4,192]{0,2,1:T(8,128)(2,1)S(1)} %copy-done.10, f32[4,256]{1,0:T(4,128)S(1)} %bitcast.164, f32[4,256,4096]{2,1,0:T(8,128)} %get-tuple-element.25, f32[4,256]{1,0:T(4,128)S(1)} %get-tuple-element.24, bf16[1,4096,4,192]{1,3,0,2:T(8,128)(2,1)} %all-gather.11.cloned.1.call-done), kind=kOutput, calls=%fused_computation.1 | convolution fusion | flops 1627389952 | bytes 31858688 | tf_op jit(solution)/shard_map/qbhd,kbhd->bhqk/dot_general | solution.py:88
  292.3 3.5 copy-done.2
  295.8 4.6 fusion.14
  301.4 3.5 fusion.23
  304.9 8.1 %fusion.95 = bf16[1,256,4,1,192]{1,4,2,3,0:T(8,128)(2,1)S(1)} fusion(bf16[4,256,4096]{2,1,0:T(8,128)(2,1)} %copy-done.2, bf16[1,4096,4,192]{1,3,0,2:T(8,128)(2,1)} %all-gather.13.cloned.1.call-done), kind=kOutput, calls=%fused_computation.83 | convolution fusion | flops 1611005952 | bytes 15073280 | tf_op jit(solution)/shard_map/bhqk,kbhd->qbhd/dot_general | solution.py:93
  313.1 52.4 %reduce-scatter.9.cloned.1.call-done = bf16[256,4,1,192]{0,3,1,2:T(8,128)(2,1)} async-done(((bf16[4096,4,1,192]{0,3,1,2:T(8,128)(2,1)}), bf16[256,4,1,192]{0,3,1,2:T(8,128)(2,1)}) %reduce-scatter.9.cloned.1.call-update) | async-done | bytes 393232 | tf_op jit(solution)/shard_map/reduce_scatter | solution.py:106
  365.5 92.3 %reduce-scatter.7.cloned.1.call-done = bf16[256,4,1,192]{0,3,1,2:T(8,128)(2,1)} async-done(((bf16[4096,4,1,192]{0,3,1,2:T(8,128)(2,1)}), bf16[256,4,1,192]{0,3,1,2:T(8,128)(2,1)}) %reduce-scatter.7.cloned.1.call-update) | async-done | bytes 393232 | tf_op jit(solution)/shard_map/reduce_scatter | solution.py:103
  457.8 5.3 fusion.18
  464.1 5.2 bitcast_convert_fusion
  470.5 2.7 convolution_convert_fusion.1
  473.2 126.5 %all-reduce.3.cloned.1.call-done = (bf16[3,1536,192]{1,2,0:T(8,128)(2,1)}, bf16[192,1536]{1,0:T(8,128)(2,1)}) async-done(((bf16[3,1536,192]{1,2,0:T(8,128)(2,1)}, bf16[192,1536]{1,0:T(8,128)(2,1)}), (bf16[3,1536,192]{1,2,0:T(8,128)(2,1)}, bf16[192,1536]{1,0:T(8,128)(2,1)})) %all-reduce.3.cloned.1.call-update) | async-done | bytes 2359312 | tf_op jit(solution)/shard_map/psum | solution.py:142
  599.7 3.8 convert_element_type.130
  604.7 53.4 %reduce-scatter.11.cloned.1.call-done = bf16[32,4,1536]{2,0,1:T(8,128)(2,1)} async-done(((bf16[256,4,1536]{2,0,1:T(8,128)(2,1)}), bf16[32,4,1536]{2,0,1:T(8,128)(2,1)}) %reduce-scatter.11.cloned.1.call-update) | async-done | bytes 393232 | tf_op jit(solution)/shard_map/reduce_scatter | solution.py:117
  659.4 47.1 %reduce-scatter.5.cloned.1.call-done = bf16[32,4,1536]{2,0,1:T(8,128)(2,1)} async-done(((bf16[256,4,1536]{2,0,1:T(8,128)(2,1)}), bf16[32,4,1536]{2,0,1:T(8,128)(2,1)}) %reduce-scatter.5.cloned.1.call-update) | async-done | bytes 393232 | tf_op jit(solution)/shard_map/reduce_scatter | solution.py:73
  711.5 2.9 fusion.60
  720.2 7.8 %collective-permute-start.2 = (bf16[2,4,1536]{2,0,1:T(2,128)(2,1)S(1)}, bf16[2,4,1536]{2,0,1:T(2,128)(2,1)S(1)}, u32[]{:S(2)}, u32[]{:S(2)}) collective-permute-start(bf16[2,4,1536]{2,0,1:T(2,128)(2,1)S(1)} %get-tuple-element.14), channel_id=1, source_target_pairs={{1,0},{2,1},{3,2},{4,3},{5,4},{6,5},{7,6},{8,7},{9,8},{10,9},{11,1... | collective-permute-start | bytes 73736 | tf_op jit(solution)/shard_map/ppermute | solution.py:18
  (76 shorter events, 47.5 us)
Async XLA Ops:
  7.2 78.7 %copy-start = (bf16[3,1536,192]{1,2,0:T(8,128)(2,1)S(1)}, bf16[3,1536,192]{1,2,0:T(8,128)(2,1)}, u32[]{:S(2)}) copy-start(bf16[3,1536,192]{1,2,0:T(8,128)(2,1)} %param.9) | copy-start | bytes 5308420
  7.2 78.7 %all-gather.7.cloned.1.call-start = ((), (), s32[]{:S(2)}) async-start(), calls=%async_computation.4 | async-start | bytes 3538944 | tf_op jit(solution)/shard_map/all_gather | solution.py:47
  8.4 12.0 %collective-permute-start.1 = (bf16[2,4,768]{2,0,1:T(2,128)(2,1)S(1)}, bf16[2,4,768]{2,0,1:T(2,128)(2,1)S(1)}, u32[]{:S(2)}, u32[]{:S(2)}) collective-permute-start(bf16[2,4,768]{2,0,1:T(2,128)(2,1)S(1)} %get-tuple-element.19), channel_id=1, source_target_pairs={{1,0},{2,1},{3,2},{4,3},{5,4},{6,5},{7,6},{8,7},{9,8},{10,9},{11,1... | collective-permute-start | bytes 36872 | tf_op jit(solution)/shard_map/ppermute | solution.py:18
  15.9 9.2 %collective-permute-start = (bf16[2,4,768]{2,0,1:T(2,128)(2,1)S(1)}, bf16[2,4,768]{2,0,1:T(2,128)(2,1)S(1)}, u32[]{:S(2)}, u32[]{:S(2)}) collective-permute-start(bf16[2,4,768]{2,0,1:T(2,128)(2,1)S(1)} %get-tuple-element.18), channel_id=1, source_target_pairs={{0,1},{1,2},{2,3},{3,4},{4,5},{5,6},{6,7},{7,8},{8,9},{9,10},{10,1... | collective-permute-start | bytes 36872 | tf_op jit(solution)/shard_map/ppermute | solution.py:15
  36.7 4.3 copy-start.11
  39.6 2.4 copy-start.3
  42.0 90.1 %all-gather.9.cloned.1.call-start = ((), (), s32[]{:S(2)}) async-start(), calls=%async_computation.6 | async-start | bytes 3538944 | tf_op jit(solution)/shard_map/all_gather | solution.py:48
  42.9 159.6 %all-gather.13.cloned.1.call-start = ((), (), s32[]{:S(2)}) async-start(), calls=%async_computation.11 | async-start | bytes 6684672 | tf_op jit(solution)/shard_map/all_gather | solution.py:56
  90.8 182.3 %all-gather.11.cloned.1.call-start = ((), (), s32[]{:S(2)}) async-start(), calls=%async_computation.10 | async-start | bytes 6684672 | tf_op jit(solution)/shard_map/all_gather | solution.py:57
  91.3 274.1 %reduce-scatter.9.cloned.1.call-start = ((), (), s32[]{:S(2)}) async-start(), calls=%async_computation.8 | async-start | bytes 6684672 | tf_op jit(solution)/shard_map/reduce_scatter | solution.py:106
  231.6 10.2 %copy-start.9 = (bf16[256,4,192]{0,2,1:T(8,128)(2,1)S(1)}, bf16[256,4,192]{0,2,1:T(8,128)(2,1)}, u32[]{:S(2)}) copy-start(bf16[256,4,192]{0,2,1:T(8,128)(2,1)} %convolution_convert_fusion.2) | copy-start | bytes 1179652
  238.5 3.3 copy-start.1
  246.4 211.4 %reduce-scatter.7.cloned.1.call-start = ((), (), s32[]{:S(2)}) async-start(), calls=%async_computation.7 | async-start | bytes 6684672 | tf_op jit(solution)/shard_map/reduce_scatter | solution.py:103
  273.1 8.9 %copy-start.10 = (bf16[256,4,192]{0,2,1:T(8,128)(2,1)S(1)}, bf16[256,4,192]{0,2,1:T(8,128)(2,1)}, u32[]{:S(2)}) copy-start(bf16[256,4,192]{0,2,1:T(8,128)(2,1)} %convolution_convert_fusion.2) | copy-start | bytes 1179652
  292.3 3.5 copy-start.2
  300.4 1.0 copy-start.8
  300.4 299.3 %all-reduce.3.cloned.1.call-start = ((), (), s32[]{:S(2)}) async-start(), calls=%async_computation.12 | async-start | bytes 4718592 | tf_op jit(solution)/shard_map/psum | solution.py:142
  313.0 144.8 %copy-start.13 = (bf16[1,256,4,1,192]{1,4,2,3,0:T(8,128)(2,1)}, bf16[1,256,4,1,192]{1,4,2,3,0:T(8,128)(2,1)S(1)}, u32[]{:S(2)}) copy-start(bf16[1,256,4,1,192]{1,4,2,3,0:T(8,128)(2,1)S(1)} %fusion.95) | copy-start | bytes 1179652
  463.1 1.0 copy-start.12
  463.2 194.9 %reduce-scatter.11.cloned.1.call-start = ((), (), s32[]{:S(2)}) async-start(), calls=%async_computation.9 | async-start | bytes 3538944 | tf_op jit(solution)/shard_map/reduce_scatter | solution.py:117
  469.4 1.1 copy-start.7
  469.4 237.0 %reduce-scatter.5.cloned.1.call-start = ((), (), s32[]{:S(2)}) async-start(), calls=%async_computation.5 | async-start | bytes 3538944 | tf_op jit(solution)/shard_map/reduce_scatter | solution.py:73
  599.7 3.8 copy-start.6
  603.5 103.0 %copy-start.4 = (bf16[32,4,1536]{2,1,0:T(4,128)(2,1)S(1)}, bf16[32,4,1536]{2,1,0:T(4,128)(2,1)}, u32[]{:S(2)}) copy-start(bf16[32,4,1536]{2,1,0:T(4,128)(2,1)} %param.11) | copy-start | bytes 1179652
  714.5 4.6 copy-start.5
  714.5 13.5 %collective-permute-start.3 = (bf16[2,4,1536]{2,0,1:T(2,128)(2,1)S(1)}, bf16[2,4,1536]{2,0,1:T(2,128)(2,1)S(1)}, u32[]{:S(2)}, u32[]{:S(2)}) collective-permute-start(bf16[2,4,1536]{2,0,1:T(2,128)(2,1)S(1)} %get-tuple-element.15), channel_id=1, source_target_pairs={{0,1},{1,2},{2,3},{3,4},{4,5},{5,6},{6,7},{7,8},{8,9},{9,10},{10,1... | collective-permute-start | bytes 73736 | tf_op jit(solution)/shard_map/ppermute | solution.py:15
  720.2 12.8 %collective-permute-start.2 = (bf16[2,4,1536]{2,0,1:T(2,128)(2,1)S(1)}, bf16[2,4,1536]{2,0,1:T(2,128)(2,1)S(1)}, u32[]{:S(2)}, u32[]{:S(2)}) collective-permute-start(bf16[2,4,1536]{2,0,1:T(2,128)(2,1)S(1)} %get-tuple-element.14), channel_id=1, source_target_pairs={{1,0},{2,1},{3,2},{4,3},{5,4},{6,5},{7,6},{8,7},{9,8},{10,9},{11,1... | collective-permute-start | bytes 73736 | tf_op jit(solution)/shard_map/ppermute | solution.py:18
Sparse Core Ops, SparseCore 0:
  42.1 43.7 all-gather.6
  88.1 43.8 all-gather.8
  134.9 67.5 all-gather.12
  205.1 67.9 all-gather.10
  277.1 88.3 reduce-scatter.8
  369.5 88.2 reduce-scatter.6
  463.3 136.3 all-reduce.2
  602.1 55.9 reduce-scatter.10
  660.5 45.8 reduce-scatter.4
where the time goes:
time: 747 us; the launch traced here: 746 us
  waiting for transfers between devices  551 us (74%)
  matrix products  98.8 us (13%)
  other arithmetic  41.8 us (6%)
  starting transfers between devices  20.3 us (3%)
  local copies, waits for them, and re-layouts  19.5 us (3%)
  between operations  14.1 us (2%)
    psum x1, waiting for transfers between devices, body(): lax.psum(part_w_qkv.astype(jnp.bfloat16), 'seq').astype(jnp.float32)  127 us
    reduce_scatter x1, waiting for transfers between devices, body(): lax.psum_scatter(key_terms.astype(jnp.bfloat16), 'seq', scatter_dimension...  92.3 us
    all_gather x1, waiting for transfers between devices, body(): lax.all_gather(key_matrix, 'seq', axis=0, tiled=True)  66.5 us
    reduce_scatter x1, waiting for transfers between devices, body(): lax.psum_scatter(jnp.einsum('itbe,ice->tbc', piece, w_qkv, preferred_elem...  53.4 us
    reduce_scatter x1, waiting for transfers between devices, body(): lax.psum_scatter(value_terms.astype(jnp.bfloat16), 'seq', scatter_dimensi...  52.4 us
    reduce_scatter x1, waiting for transfers between devices, body(): lax.psum_scatter(jnp.einsum('tbe,ec->tbc', piece, w_out, preferred_elemen...  47.1 us
    all_gather x1, waiting for transfers between devices, body(): normed_rows = lax.all_gather(normed, 'head', axis=0, tiled=True)  43 us
    all_gather x1, waiting for transfers between devices, body(): grad_rows = lax.all_gather(grad_out, 'head', axis=0, tiled=True)  40.5 us
  transfers between devices with their start and end apart: 13, of which 10 were waited for; matrix products, arithmetic and copies ran while one was open for 15% of the time, Pallas kernels for 0%

commit v1 on v0

--- a/solution.py
+++ b/solution.py
@@ -44,8 +44,11 @@
     skip_wide = skip.astype(jnp.float32)
     inv_rms = lax.rsqrt(jnp.mean(skip_wide * skip_wide, axis=-1, keepdims=True) + 1e-06)
     normed = (skip_wide * inv_rms * norm_gain).astype(jnp.bfloat16)
-    normed_rows = lax.all_gather(normed, "head", axis=0, tiled=True)
-    grad_rows = lax.all_gather(grad_out, "head", axis=0, tiled=True)
+    normed_rows, grad_rows = jnp.split(
+        lax.all_gather(jnp.concatenate([normed, grad_out], axis=1), "head", axis=0, tiled=True),
+        [normed.shape[1]],
+        axis=1,
+    )
     tower_rows = normed_rows.shape[0]
     qkv = jnp.einsum(
         "tbc,ice->itbe", normed_rows, w_qkv, preferred_element_type=jnp.float32

time: 747 us -> 733 us (0.981)
  waiting for transfers between devices: 551 us -> 535 us
    all_gather x2 -> x1, waiting for transfers between devices: 83.4 us -> 72.8 us  [body(): lax.all_gather(jnp.concatenate([normed, grad_out], axis=1), 'head', axis=...]
  transfers between devices with their start and end apart: 13 -> 12, of which waited for: 10 -> 9; matrix products, arithmetic and copies ran while one was open for 15% -> 15% of each run, Pallas kernels for 0% -> 0%
where the time goes in v1:
time: 733 us; the launch traced here: 731 us
  waiting for transfers between devices  535 us (73%)
  matrix products  98.9 us (13%)
  other arithmetic  42.8 us (6%)
  starting transfers between devices  20.4 us (3%)
  local copies, waits for them, and re-layouts  19.5 us (3%)
  between operations  14.4 us (2%)
    psum x1, waiting for transfers between devices, body(): lax.psum(part_w_qkv.astype(jnp.bfloat16), 'seq').astype(jnp.float32)  127 us
    reduce_scatter x1, waiting for transfers between devices, body(): lax.psum_scatter(key_terms.astype(jnp.bfloat16), 'seq', scatter_dimension...  92.3 us
    all_gather x1, waiting for transfers between devices, body(): lax.all_gather(jnp.concatenate([normed, grad_out], axis=1), 'head', axis=...  72.8 us
    all_gather x1, waiting for transfers between devices, body(): lax.all_gather(key_matrix, 'seq', axis=0, tiled=True)  61.8 us
    reduce_scatter x1, waiting for transfers between devices, body(): lax.psum_scatter(jnp.einsum('itbe,ice->tbc', piece, w_qkv, preferred_elem...  53.4 us
    reduce_scatter x1, waiting for transfers between devices, body(): lax.psum_scatter(value_terms.astype(jnp.bfloat16), 'seq', scatter_dimensi...  52.4 us
    reduce_scatter x1, waiting for transfers between devices, body(): lax.psum_scatter(jnp.einsum('tbe,ec->tbc', piece, w_out, preferred_elemen...  46.4 us
    all_gather x1, waiting for transfers between devices, body(): lax.all_gather(value_matrix, 'seq', axis=0, tiled=True)  26.7 us
  transfers between devices with their start and end apart: 12, of which 9 were waited for; matrix products, arithmetic and copies ran while one was open for 15% of the time, Pallas kernels for 0%

profile of v1, /device:TPU:16, one launch (start us, length us, event | category | flops | bytes accessed | tf_op | source)
XLA Modules:
  0.0 730.9 jit_solution(2438587712720437097)
XLA Ops:
  8.4 7.6 %collective-permute-start.1 = (bf16[2,4,768]{2,0,1:T(2,128)(2,1)S(1)}, bf16[2,4,768]{2,0,1:T(2,128)(2,1)S(1)}, u32[]{:S(2)}, u32[]{:S(2)}) collective-permute-start(bf16[2,4,768]{2,0,1:T(2,128)(2,1)S(1)} %get-tuple-element.19), channel_id=1, source_target_pairs={{1,0},{2,1},{3,2},{4,3},{5,4},{6,5},{7,6},{8,7},{9,8},{10,9},{11,1... | collective-permute-start | bytes 36872 | tf_op jit(solution)/shard_map/ppermute | solution.py:18
  18.0 2.6 fusion.42
  30.2 4.4 multiply_multiply_fusion.2
  36.9 2.9 reduce_sum.47
  43.3 72.8 %all-gather.6.cloned.1.call-done = bf16[256,8,1536]{2,0,1:T(8,128)(2,1)} async-done(((bf16[32,8,1536]{2,0,1:T(8,128)(2,1)}), bf16[256,8,1536]{2,0,1:T(8,128)(2,1)}) %all-gather.6.cloned.1.call-update) | async-done | bytes 6291472 | tf_op jit(solution)/shard_map/all_gather | solution.py:48
  116.1 3.9 fusion.75
  121.9 3.9 convolution_convert_fusion.2
  125.9 61.8 %all-gather.10.cloned.1.call-done = bf16[1,4096,4,192]{1,3,0,2:T(8,128)(2,1)} async-done(((bf16[1,256,4,192]{1,3,0,2:T(8,128)(2,1)}), bf16[1,4096,4,192]{1,3,0,2:T(8,128)(2,1)}) %all-gather.10.cloned.1.call-update) | async-done | bytes 6291472 | tf_op jit(solution)/shard_map/all_gather | solution.py:59
  187.7 10.9 %fusion.8 = f32[4,256,4096]{2,1,0:T(8,128)} fusion(bf16[1,4096,4,192]{1,3,0,2:T(8,128)(2,1)} %all-gather.10.cloned.1.call-done, bf16[3,256,4,192]{1,3,0,2:T(8,128)(2,1)S(1)} %fusion.75), kind=kOutput, calls=%fused_computation.13 | convolution fusion | flops 1610612736 | bytes 23461888 | tf_op jit(solution)/shard_map/qbhd,kbhd->bhqk/dot_general | solution.py:63
  198.6 18.2 %fusion.150 = (f32[4,256]{1,0:T(4,128)S(1)}, f32[4,256,4096]{2,1,0:T(8,128)}) fusion(f32[4,256,4096]{2,1,0:T(8,128)} %fusion.8), kind=kOutput, calls=%fused_computation.150 | output fusion | flops 16781312 | bytes 33558528 | tf_op jit(solution)/shard_map/sub | solution.py:67
  216.7 6.9 fusion.5
  223.7 3.3 copy-done.1
  227.0 4.5 fusion.13
  231.8 26.7 %all-gather.8.cloned.1.call-done = bf16[1,4096,4,192]{1,3,0,2:T(8,128)(2,1)} async-done(((bf16[1,256,4,192]{1,3,0,2:T(8,128)(2,1)}), bf16[1,4096,4,192]{1,3,0,2:T(8,128)(2,1)}) %all-gather.8.cloned.1.call-update) | async-done | bytes 6291472 | tf_op jit(solution)/shard_map/all_gather | solution.py:60
  258.5 8.9 %fusion.124 = (f32[256,4]{0,1:T(4,128)S(1)}, bf16[256,4,1,192]{0,3,1,2:T(8,128)(2,1)}) fusion(bf16[256,4,192]{0,2,1:T(8,128)(2,1)} %convolution_convert_fusion.2, bf16[4,256,4096]{2,1,0:T(8,128)(2,1)} %copy-done.1, bf16[1,4096,4,192]{1,3,0,2:T(8,128)(2,1)} %all-gather.8.cloned.1.call-done), kind=kOutput, calls=%fused_computation.115 | convolution fusion | flops 1611398144 | bytes 15470592 | tf_op jit(solution)/shard_map/bhqk,kbhd->qbhd/dot_general | solution.py:71
  267.4 10.3 %multiply_convert_fusion = bf16[4,256,4096]{2,1,0:T(8,128)(2,1)S(1)} fusion(bf16[256,4,192]{0,2,1:T(8,128)(2,1)S(1)} %copy-done.10, f32[4,256]{1,0:T(4,128)S(1)} %bitcast.163, f32[4,256,4096]{2,1,0:T(8,128)} %get-tuple-element.25, f32[4,256]{1,0:T(4,128)S(1)} %get-tuple-element.24, bf16[1,4096,4,192]{1,3,0,2:T(8,128)(2,1)} %all-gather.8.cloned.1.call-done), kind=kOutput, calls=%fused_computation.1 | convolution fusion | flops 1627389952 | bytes 31858688 | tf_op jit(solution)/shard_map/qbhd,kbhd->bhqk/dot_general | solution.py:91
  277.7 3.5 copy-done.2
  281.2 4.6 fusion.14
  286.8 3.5 fusion.30
  290.4 8.1 %fusion.104 = bf16[1,256,4,1,192]{1,4,2,3,0:T(8,128)(2,1)S(1)} fusion(bf16[4,256,4096]{2,1,0:T(8,128)(2,1)} %copy-done.2, bf16[1,4096,4,192]{1,3,0,2:T(8,128)(2,1)} %all-gather.10.cloned.1.call-done), kind=kOutput, calls=%fused_computation.87 | convolution fusion | flops 1611005952 | bytes 15073280 | tf_op jit(solution)/shard_map/bhqk,kbhd->qbhd/dot_general | solution.py:96
  298.5 52.4 %reduce-scatter.9.cloned.1.call-done = bf16[256,4,1,192]{0,3,1,2:T(8,128)(2,1)} async-done(((bf16[4096,4,1,192]{0,3,1,2:T(8,128)(2,1)}), bf16[256,4,1,192]{0,3,1,2:T(8,128)(2,1)}) %reduce-scatter.9.cloned.1.call-update) | async-done | bytes 393232 | tf_op jit(solution)/shard_map/reduce_scatter | solution.py:109
  350.9 92.3 %reduce-scatter.7.cloned.1.call-done = bf16[256,4,1,192]{0,3,1,2:T(8,128)(2,1)} async-done(((bf16[4096,4,1,192]{0,3,1,2:T(8,128)(2,1)}), bf16[256,4,1,192]{0,3,1,2:T(8,128)(2,1)}) %reduce-scatter.7.cloned.1.call-update) | async-done | bytes 393232 | tf_op jit(solution)/shard_map/reduce_scatter | solution.py:106
  443.2 5.3 fusion.20
  449.5 5.2 bitcast_convert_fusion
  455.8 2.7 convolution_convert_fusion.1
  458.6 126.7 %all-reduce.3.cloned.1.call-done = (bf16[3,1536,192]{1,2,0:T(8,128)(2,1)}, bf16[192,1536]{1,0:T(8,128)(2,1)}) async-done(((bf16[3,1536,192]{1,2,0:T(8,128)(2,1)}, bf16[192,1536]{1,0:T(8,128)(2,1)}), (bf16[3,1536,192]{1,2,0:T(8,128)(2,1)}, bf16[192,1536]{1,0:T(8,128)(2,1)})) %all-reduce.3.cloned.1.call-update) | async-done | bytes 2359312 | tf_op jit(solution)/shard_map/psum | solution.py:145
  585.3 3.8 convert_element_type.130
  590.2 53.4 %reduce-scatter.11.cloned.1.call-done = bf16[32,4,1536]{2,0,1:T(8,128)(2,1)} async-done(((bf16[256,4,1536]{2,0,1:T(8,128)(2,1)}), bf16[32,4,1536]{2,0,1:T(8,128)(2,1)}) %reduce-scatter.11.cloned.1.call-update) | async-done | bytes 393232 | tf_op jit(solution)/shard_map/reduce_scatter | solution.py:120
  645.0 46.4 %reduce-scatter.5.cloned.1.call-done = bf16[32,4,1536]{2,0,1:T(8,128)(2,1)} async-done(((bf16[256,4,1536]{2,0,1:T(8,128)(2,1)}), bf16[32,4,1536]{2,0,1:T(8,128)(2,1)}) %reduce-scatter.5.cloned.1.call-update) | async-done | bytes 393232 | tf_op jit(solution)/shard_map/reduce_scatter | solution.py:76
  696.4 2.9 fusion.69
  699.4 2.9 collective-permute-start.3
  705.8 7.0 collective-permute-start.2
  (74 shorter events, 45.9 us)
Async XLA Ops:
  7.2 108.9 %copy-start = (bf16[3,1536,192]{1,2,0:T(8,128)(2,1)S(1)}, bf16[3,1536,192]{1,2,0:T(8,128)(2,1)}, u32[]{:S(2)}) copy-start(bf16[3,1536,192]{1,2,0:T(8,128)(2,1)} %param.9) | copy-start | bytes 5308420
  7.2 108.9 %all-gather.6.cloned.1.call-start = ((), (), s32[]{:S(2)}) async-start(), calls=%async_computation.4 | async-start | bytes 7077888 | tf_op jit(solution)/shard_map/all_gather | solution.py:48
  8.4 12.2 %copy-start.3 = (bf16[32,4,1536]{2,1,0:T(4,128)(2,1)S(1)}, bf16[32,4,1536]{2,1,0:T(4,128)(2,1)}, u32[]{:S(2)}) copy-start(bf16[32,4,1536]{2,1,0:T(4,128)(2,1)} %param.11) | copy-start | bytes 1179652
  8.4 12.9 %collective-permute-start.1 = (bf16[2,4,768]{2,0,1:T(2,128)(2,1)S(1)}, bf16[2,4,768]{2,0,1:T(2,128)(2,1)S(1)}, u32[]{:S(2)}, u32[]{:S(2)}) collective-permute-start(bf16[2,4,768]{2,0,1:T(2,128)(2,1)S(1)} %get-tuple-element.19), channel_id=1, source_target_pairs={{1,0},{2,1},{3,2},{4,3},{5,4},{6,5},{7,6},{8,7},{9,8},{10,9},{11,1... | collective-permute-start | bytes 36872 | tf_op jit(solution)/shard_map/ppermute | solution.py:18
  16.1 9.2 %collective-permute-start = (bf16[2,4,768]{2,0,1:T(2,128)(2,1)S(1)}, bf16[2,4,768]{2,0,1:T(2,128)(2,1)S(1)}, u32[]{:S(2)}, u32[]{:S(2)}) collective-permute-start(bf16[2,4,768]{2,0,1:T(2,128)(2,1)S(1)} %get-tuple-element.18), channel_id=1, source_target_pairs={{0,1},{1,2},{2,3},{3,4},{4,5},{5,6},{6,7},{7,8},{8,9},{9,10},{10,1... | collective-permute-start | bytes 36872 | tf_op jit(solution)/shard_map/ppermute | solution.py:15
  36.8 4.3 copy-start.11
  43.2 144.4 %all-gather.10.cloned.1.call-start = ((), (), s32[]{:S(2)}) async-start(), calls=%async_computation.10 | async-start | bytes 6684672 | tf_op jit(solution)/shard_map/all_gather | solution.py:59
  121.0 137.5 %all-gather.8.cloned.1.call-start = ((), (), s32[]{:S(2)}) async-start(), calls=%async_computation.9 | async-start | bytes 6684672 | tf_op jit(solution)/shard_map/all_gather | solution.py:60
  121.7 229.2 %reduce-scatter.9.cloned.1.call-start = ((), (), s32[]{:S(2)}) async-start(), calls=%async_computation.7 | async-start | bytes 6684672 | tf_op jit(solution)/shard_map/reduce_scatter | solution.py:109
  216.7 10.2 %copy-start.9 = (bf16[256,4,192]{0,2,1:T(8,128)(2,1)S(1)}, bf16[256,4,192]{0,2,1:T(8,128)(2,1)}, u32[]{:S(2)}) copy-start(bf16[256,4,192]{0,2,1:T(8,128)(2,1)} %convolution_convert_fusion.2) | copy-start | bytes 1179652
  223.7 3.3 copy-start.1
  231.5 211.7 %reduce-scatter.7.cloned.1.call-start = ((), (), s32[]{:S(2)}) async-start(), calls=%async_computation.6 | async-start | bytes 6684672 | tf_op jit(solution)/shard_map/reduce_scatter | solution.py:106
  258.5 8.9 %copy-start.10 = (bf16[256,4,192]{0,2,1:T(8,128)(2,1)S(1)}, bf16[256,4,192]{0,2,1:T(8,128)(2,1)}, u32[]{:S(2)}) copy-start(bf16[256,4,192]{0,2,1:T(8,128)(2,1)} %convolution_convert_fusion.2) | copy-start | bytes 1179652
  277.7 3.5 copy-start.2
  285.8 1.0 copy-start.8
  285.8 299.5 %all-reduce.3.cloned.1.call-start = ((), (), s32[]{:S(2)}) async-start(), calls=%async_computation.11 | async-start | bytes 4718592 | tf_op jit(solution)/shard_map/psum | solution.py:145
  298.5 144.7 %copy-start.13 = (bf16[1,256,4,1,192]{1,4,2,3,0:T(8,128)(2,1)}, bf16[1,256,4,1,192]{1,4,2,3,0:T(8,128)(2,1)S(1)}, u32[]{:S(2)}) copy-start(bf16[1,256,4,1,192]{1,4,2,3,0:T(8,128)(2,1)S(1)} %fusion.104) | copy-start | bytes 1179652
  448.5 1.0 copy-start.12
  448.6 195.1 %reduce-scatter.11.cloned.1.call-start = ((), (), s32[]{:S(2)}) async-start(), calls=%async_computation.8 | async-start | bytes 3538944 | tf_op jit(solution)/shard_map/reduce_scatter | solution.py:120
  454.8 1.1 copy-start.7
  454.8 236.6 %reduce-scatter.5.cloned.1.call-start = ((), (), s32[]{:S(2)}) async-start(), calls=%async_computation.5 | async-start | bytes 3538944 | tf_op jit(solution)/shard_map/reduce_scatter | solution.py:76
  585.3 3.8 copy-start.6
  589.1 102.3 %copy-start.4 = (bf16[32,4,1536]{2,1,0:T(4,128)(2,1)S(1)}, bf16[32,4,1536]{2,1,0:T(4,128)(2,1)}, u32[]{:S(2)}) copy-start(bf16[32,4,1536]{2,1,0:T(4,128)(2,1)} %param.11) | copy-start | bytes 1179652
  699.4 5.4 copy-start.5
  699.4 13.5 %collective-permute-start.3 = (bf16[2,4,1536]{2,0,1:T(2,128)(2,1)S(1)}, bf16[2,4,1536]{2,0,1:T(2,128)(2,1)S(1)}, u32[]{:S(2)}, u32[]{:S(2)}) collective-permute-start(bf16[2,4,1536]{2,0,1:T(2,128)(2,1)S(1)} %get-tuple-element.15), channel_id=1, source_target_pairs={{0,1},{1,2},{2,3},{3,4},{4,5},{5,6},{6,7},{7,8},{8,9},{9,10},{10,1... | collective-permute-start | bytes 73736 | tf_op jit(solution)/shard_map/ppermute | solution.py:15
  705.8 12.1 %collective-permute-start.2 = (bf16[2,4,1536]{2,0,1:T(2,128)(2,1)S(1)}, bf16[2,4,1536]{2,0,1:T(2,128)(2,1)S(1)}, u32[]{:S(2)}, u32[]{:S(2)}) collective-permute-start(bf16[2,4,1536]{2,0,1:T(2,128)(2,1)S(1)} %get-tuple-element.14), channel_id=1, source_target_pairs={{1,0},{2,1},{3,2},{4,3},{5,4},{6,5},{7,6},{8,7},{9,8},{10,9},{11,1... | collective-permute-start | bytes 73736 | tf_op jit(solution)/shard_map/ppermute | solution.py:18
Sparse Core Ops, SparseCore 0:
  43.4 72.6 all-gather.5
  121.1 66.5 all-gather.9
  190.5 67.9 all-gather.7
  262.5 88.3 reduce-scatter.8
  354.9 88.2 reduce-scatter.6
  448.7 136.5 all-reduce.2
  587.7 55.9 reduce-scatter.10
  646.1 45.2 reduce-scatter.4
